TPU v7x, 512 devices: a whole 4x4x16 slice. The times are simulated.
512 devices in a mesh: seq: 16 (over x, y), chan: 32 (over z, core).
Axes of the slice: x: 4, y: 4, z: 16, core: 2. Of those that a mesh axis runs over, the one named last changes fastest.
Arguments:
- grad_out: bfloat16 [8192, 4096], P('seq', 'chan'), may hold values from -6 to 6
- activation: bfloat16 [8192, 4096], P('seq', 'chan'), may hold values from -6 to 6
- residues: float32 [4096, 16], P('chan'), may hold values from -1.5 to 1.5
- decay: float32 [4096, 16], P('chan'), may hold values from 2.4414063e-05 to 0.0333333333
- skip: float32 [4096], P('chan'), may hold values from -3 to 3
- in_weight: bfloat16 [4096, 4096], P('chan'), may hold values from -0.09375 to 0.09375
Outputs:
- input_grad: bfloat16 [8192, 4096], P('seq', 'chan')
- residue_grad: float32 [4096, 16], P('chan')
All inputs are finite; a program needn't handle non-finite values.
Results may differ from a plain program's by a relative error of at most 0.012.
Values may be sent and summed in bfloat16 or wider, within the bound.
A program may use at most 64 MiB of HBM per device.

v0:
```python
import functools
import math

import jax
import jax.numpy as jnp
from jax import lax
from jax.experimental import pallas as pl
from jax.experimental.pallas import tpu as pltpu
from jax.sharding import PartitionSpec as P

MESH = pl.DeviceIdType.MESH
SUB = 8
PIECES = 4


def kernel(
    nseq,
    nz,
    scale_len,
    g_hbm,
    act_hbm,
    res_hbm,
    dec_hbm,
    skip_hbm,
    w_hbm,
    out_ref,
    rg_ref,
    gath,
    w_v,
    g_b,
    act_b,
    res_v,
    dec_v,
    skip_v,
    g_f,
    act_f,
    y_f,
    acc,
    nat,
    a_bc,
    r_bc,
    z_bc,
    l_bc,
    b_bc,
    c_bc,
    dec_t,
    states,
    parts,
    load_sem,
    st_send,
    st_recv,
    pt_send,
    pt_recv,
    up_send,
    up_recv,
    dn_send,
    dn_recv,
    pr_send,
    pr_recv,
):
    rows, lanes = g_b.shape
    orders = dec_v.shape[1]
    steps = rows // SUB
    half = nz // 2
    piece = rows // PIECES
    me_s = lax.axis_index("seq")
    me_c = lax.axis_index("chan")
    me_z = me_c // 2
    core = me_c % 2
    partner = me_z * 2 + (1 - core)
    above = ((me_z + 1) % nz) * 2 + core
    below = ((me_z + nz - 1) % nz) * 2 + core

    def load(src, dst, index):
        return pltpu.make_async_copy(src, dst, load_sem.at[index])

    loads = [
        load(g_hbm, g_b, 0),
        load(dec_hbm, dec_v, 1),
        load(res_hbm, res_v, 2),
        load(skip_hbm, skip_v, 3),
        load(act_hbm, act_b, 4),
        load(w_hbm, w_v, 5),
    ]
    barrier = pltpu.get_barrier_semaphore()
    for hop in range(1, nseq):
        pl.semaphore_signal(
            barrier, inc=1, device_id=((me_s + hop) % nseq, me_c), device_id_type=MESH
        )
    for other in (partner, above, below):
        pl.semaphore_signal(barrier, inc=1, device_id=(me_s, other), device_id_type=MESH)
    for copy in loads:
        copy.start()

    loads[1].wait()
    loads[2].wait()
    loads[3].wait()
    decay_t = jnp.transpose(dec_v[...])
    dec_t[...] = decay_t
    weight_t = jnp.sqrt(2.0 * decay_t)
    strength_t = jnp.transpose(res_v[...]) * weight_t
    pole_t = jnp.exp(-decay_t)
    for n in range(orders):
        a_bc[n] = jnp.broadcast_to(pole_t[n : n + 1], (SUB, lanes))
        r_bc[n] = jnp.broadcast_to(strength_t[n : n + 1], (SUB, lanes))
    acc[...] = jnp.zeros_like(acc)

    loads[0].wait()
    loads[4].wait()
    g_f[...] = g_b[...].astype(jnp.float32)
    act_f[...] = act_b[...].astype(jnp.float32)

    zero = jnp.zeros((SUB, lanes), jnp.float32)
    skip_row = jnp.broadcast_to(skip_v[...], (SUB, lanes))
    group = orders // 2
    unroll = 2
    for part in range(2):
        chosen = range(part * group, (part + 1) * group)
        poles = [a_bc[n] for n in chosen]
        gains = [r_bc[n] for n in chosen]

        def scan(index, carry, poles=poles, gains=gains, part=part):
            state, total = list(carry[0]), list(carry[1])
            for inner in range(unroll):
                k = index * unroll + inner
                g_row = g_f[pl.ds(steps - 1 - k, SUB, stride=steps), :]
                act_row = act_f[pl.ds(steps - 1 - k, SUB, stride=steps), :]
                where = pl.ds(pl.multiple_of(k * SUB, SUB), SUB)
                y = skip_row * g_row if part == 0 else y_f[where, :]
                terms = []
                for m in range(group):
                    state[m] = g_row + poles[m] * state[m]
                    terms.append(gains[m] * state[m])
                    total[m] = total[m] + act_row * state[m]
                while len(terms) > 1:
                    terms = [terms[i] + terms[i + 1] for i in range(0, len(terms), 2)]
                y_f[where, :] = y + terms[0]
            return tuple(state), tuple(total)

        state, total = lax.fori_loop(
            0, steps // unroll, scan, ((zero,) * group, (zero,) * group)
        )
        for m, n in enumerate(chosen):
            z_bc[n] = state[m]
            l_bc[n] = total[m]

    row = lax.broadcasted_iota(jnp.int32, (SUB, lanes), 0)
    for n in range(orders):
        rate = jnp.broadcast_to(dec_t[n : n + 1, :], (SUB, lanes))
        state = z_bc[n]
        shift = 1
        while shift < SUB:
            moved = jnp.where(row < SUB - shift, pltpu.roll(state, SUB - shift, 0), 0.0)
            state = state + jnp.exp(rate * float(-steps * shift)) * moved
            shift *= 2
        states[me_s, n : n + 1, :] = state[0:1]
        z_bc[n] = jnp.where(row < SUB - 1, pltpu.roll(state, SUB - 1, 0), 0.0)

    pl.semaphore_wait(barrier, nseq - 1 + 3)

    def to_peer(buffer, send, recv, hop):
        peer = (me_s + hop) % nseq
        return pltpu.make_async_remote_copy(
            src_ref=buffer.at[me_s],
            dst_ref=buffer.at[me_s],
            send_sem=send.at[hop],
            recv_sem=recv.at[me_s],
            device_id=(peer, me_c),
            device_id_type=MESH,
        )

    def from_peer(buffer, send, recv, hop):
        peer = (me_s + hop) % nseq
        return pltpu.make_async_remote_copy(
            src_ref=buffer.at[peer],
            dst_ref=buffer.at[peer],
            send_sem=send.at[hop],
            recv_sem=recv.at[peer],
            device_id=(peer, me_c),
            device_id_type=MESH,
        )

    for hop in range(1, nseq):
        to_peer(states, st_send, st_recv, hop).start()

    def weigh(index, carry):
        carry = list(carry)
        for inner in range(unroll):
            j = index * unroll + inner
            act_row = act_f[pl.ds(j, SUB, stride=steps), :]
            for n in range(orders):
                carry[n] = a_bc[n] * (carry[n] + act_row)
        return tuple(carry)

    weights = lax.fori_loop(0, steps // unroll, weigh, (zero,) * orders)
    distance = (SUB - 1 - row).astype(jnp.float32) * float(steps)
    for n in range(orders):
        b_bc[n] = weights[n]
        rate = jnp.broadcast_to(dec_t[n : n + 1, :], (SUB, lanes))
        c_bc[n] = jnp.exp(-rate * distance)
    block_pole = jnp.exp(dec_t[...] * float(-rows))

    for hop in range(1, nseq):
        from_peer(states, st_send, st_recv, hop).wait_recv()
    enter = jnp.zeros((orders, lanes), jnp.float32)
    for later in range(nseq - 1, 0, -1):
        enter = jnp.where(later > me_s, states[later] + block_pole * enter, enter)
    for n in range(orders):
        c_bc[n] = z_bc[n] + c_bc[n] * jnp.broadcast_to(enter[n : n + 1], (SUB, lanes))

    def rows_of(p):
        return pl.ds(pl.multiple_of(p * piece, piece), piece)

    def ring(slot, s, p, send, recv, to):
        view = gath.at[slot, rows_of(p), :]
        return pltpu.make_async_remote_copy(
            src_ref=view,
            dst_ref=view,
            send_sem=send.at[s, p],
            recv_sem=recv.at[s, p],
            device_id=(me_s, to),
            device_id_type=MESH,
        )

    def go_up(slot, s, p):
        return ring(slot, s, p, up_send, up_recv, above)

    def go_dn(slot, s, p):
        return ring(slot, s, p, dn_send, dn_recv, below)

    def across(slot, d, s, p):
        view = gath.at[slot, rows_of(p), :]
        return pltpu.make_async_remote_copy(
            src_ref=view,
            dst_ref=view,
            send_sem=pr_send.at[d, s, p],
            recv_sem=pr_recv.at[d, s, p],
            device_id=(me_s, partner),
            device_id_type=MESH,
        )

    def chip_up(s):
        return (me_z + nz - s) % nz

    def chip_dn(s):
        return (me_z + s) % nz

    poles = [a_bc[n] for n in range(orders)]
    entering = tuple(r_bc[n] * c_bc[n] for n in range(orders))

    def finish(p, carry):
        def pair(index, carry):
            ys = []
            for inner in range(2):
                k = p * (piece // SUB) + index * 2 + inner
                carry = [poles[n] * carry[n] for n in range(orders)]
                terms = list(carry)
                while len(terms) > 1:
                    terms = [terms[i] + terms[i + 1] for i in range(0, len(terms), 2)]
                ys.append(y_f[pl.ds(pl.multiple_of(k * SUB, SUB), SUB), :] + terms[0])
            start = pl.multiple_of(p * piece + index * 2 * SUB, 2 * SUB)
            both = jnp.concatenate(ys, axis=0).astype(jnp.bfloat16)
            gath[me_c, pl.ds(start, 2 * SUB), :] = both
            return tuple(carry)

        carry = lax.fori_loop(0, piece // SUB // 2, pair, carry)
        go_up(me_c, 1, p).start()
        go_dn(me_c, 1, p).start()
        across(me_c, 0, 0, p).start()
        return carry

    lax.fori_loop(0, PIECES, finish, entering)

    for n in range(orders):
        parts[me_s, n : n + 1, :] = jnp.sum(
            l_bc[n] + b_bc[n] * c_bc[n], axis=0, keepdims=True
        )
    for hop in range(1, nseq):
        to_peer(parts, pt_send, pt_recv, hop).start()

    def multiply(chip, h):
        where = pl.ds(h * (rows // 2), rows // 2)
        block = jnp.concatenate([gath[chip * 2, where, :], gath[chip * 2 + 1, where, :]], axis=1)
        columns = pl.ds(pl.multiple_of(chip * 2 * lanes, 2 * lanes), 2 * lanes)
        acc[where, :] += lax.dot_general(
            block, w_v[:, columns], (((1,), (1,)), ((), ())), preferred_element_type=jnp.float32
        )

    def wait_partner(chip, d, s, h):
        slot = chip * 2 + (1 - core)
        for p in range(h * PIECES // 2, (h + 1) * PIECES // 2):
            across(slot, d, s, p).wait_recv()

    loads[5].wait()

    def ring_step(s, _):
        up = chip_up(s) * 2 + core
        dn = chip_dn(s) * 2 + core
        for p in range(PIECES):
            go_up(up, s, p).wait_recv()
            if p < PIECES // 2:
                go_up(up, s + 1, p).start()
            else:
                @pl.when(s < half - 1)
                def _():
                    go_up(up, s + 1, p).start()
            across(up, 0, s, p).start()
            go_dn(dn, s, p).wait_recv()
            if p >= PIECES // 2:
                go_dn(dn, s + 1, p).start()
            else:
                @pl.when(s < half - 1)
                def _():
                    go_dn(dn, s + 1, p).start()
            across(dn, 1, s, p).start()
            if p < 2:
                wait_partner(chip_up(s - 1), 0, s - 1, p)
                multiply(chip_up(s - 1), p)
            elif p < 4:
                @pl.when(s >= 2)
                def _():
                    wait_partner(chip_dn(s - 1), 1, s - 1, p - 2)
                    multiply(chip_dn(s - 1), p - 2)
        return 0

    lax.fori_loop(1, half, ring_step, 0)

    far = chip_up(half)
    near_up, near_dn = chip_up(half - 1), chip_dn(half - 1)
    for i in range(PIECES // 2):
        go_up(far * 2 + core, half, i).wait_recv()
        across(far * 2 + core, 0, half, i).start()
        go_dn(far * 2 + core, half, i + PIECES // 2).wait_recv()
        across(far * 2 + core, 0, half, i + PIECES // 2).start()
        wait_partner(near_up, 0, half - 1, i)
        multiply(near_up, i)
    for i in range(2):
        wait_partner(near_dn, 1, half - 1, i)
        multiply(near_dn, i)

    for hop in range(1, nseq):
        from_peer(parts, pt_send, pt_recv, hop).wait_recv()
    total = parts[0]
    for other in range(1, nseq):
        total = total + parts[other]
    total = total * jnp.sqrt(2.0 * dec_t[...]) * scale_len
    rg_ref[...] = jnp.transpose(total)

    for i in range(2):
        wait_partner(far, 0, half, i)
        multiply(far, i)

    for k in range(steps):
        nat[pl.ds(steps - 1 - k, SUB, stride=steps), :] = acc[k * SUB : (k + 1) * SUB, :]
    out_ref[...] = nat[...].astype(out_ref.dtype)

    for hop in range(1, nseq):
        to_peer(states, st_send, st_recv, hop).wait_send()
        to_peer(parts, pt_send, pt_recv, hop).wait_send()
    for p in range(PIECES):
        across(me_c, 0, 0, p).wait_send()

    def drain(s, _):
        for p in range(PIECES):
            go_up(me_c, s, p).wait_send()
            go_dn(me_c, s, p).wait_send()
            across(me_c, 0, s, p).wait_send()
            across(me_c, 1, s, p).wait_send()
        return 0

    lax.fori_loop(1, half, drain, 0)
    for p in range(PIECES):
        across(me_c, 0, half, p).wait_send()
        if p < PIECES // 2:
            go_up(me_c, half, p).wait_send()
        else:
            go_dn(me_c, half, p).wait_send()


def per_device(nseq, nz, grad_out, activation, residues, decay, skip, in_weight):
    rows, lanes = grad_out.shape
    orders = decay.shape[1]
    features, width = in_weight.shape
    f32, bf16 = jnp.float32, jnp.bfloat16
    half = nz // 2
    dma = pltpu.SemaphoreType.DMA
    any_spec = pl.BlockSpec(memory_space=pl.ANY)
    vmem_spec = pl.BlockSpec(memory_space=pltpu.VMEM)
    spread = pltpu.VMEM((orders, SUB, lanes), f32)
    return pl.pallas_call(
        functools.partial(kernel, nseq, nz, 1.0 / math.sqrt(nseq * rows)),
        out_shape=(
            jax.ShapeDtypeStruct((rows, features), bf16),
            jax.ShapeDtypeStruct((lanes, orders), f32),
        ),
        in_specs=[any_spec] * 6,
        out_specs=(vmem_spec, vmem_spec),
        scratch_shapes=[
            pltpu.VMEM((nz * 2, rows, lanes), bf16),
            pltpu.VMEM((features, width), bf16),
            pltpu.VMEM((rows, lanes), bf16),
            pltpu.VMEM((rows, lanes), bf16),
            pltpu.VMEM((lanes, orders), f32),
            pltpu.VMEM((lanes, orders), f32),
            pltpu.VMEM((1, lanes), f32),
            pltpu.VMEM((rows, lanes), f32),
            pltpu.VMEM((rows, lanes), f32),
            pltpu.VMEM((rows, lanes), f32),
            pltpu.VMEM((rows, features), f32),
            pltpu.VMEM((rows, features), f32),
            spread,
            spread,
            spread,
            spread,
            spread,
            spread,
            pltpu.VMEM((orders, lanes), f32),
            pltpu.VMEM((nseq, orders, lanes), f32),
            pltpu.VMEM((nseq, orders, lanes), f32),
            dma((6,)),
            dma((nseq,)),
            dma((nseq,)),
            dma((nseq,)),
            dma((nseq,)),
            dma((half + 1, PIECES)),
            dma((half + 1, PIECES)),
            dma((half + 1, PIECES)),
            dma((half + 1, PIECES)),
            dma((2, half + 1, PIECES)),
            dma((2, half + 1, PIECES)),
        ],
        compiler_params=pltpu.CompilerParams(
            collective_id=0, has_side_effects=True, vmem_limit_bytes=40 * 2**20
        ),
        name="modal_backward",
    )(grad_out, activation, residues, decay, skip.reshape(1, lanes), in_weight)


def solution(mesh):
    nseq = mesh.shape["seq"]
    nz = mesh.shape["chan"] // 2
    return jax.shard_map(
        functools.partial(per_device, nseq, nz),
        mesh=mesh,
        in_specs=(
            P("seq", "chan"),
            P("seq", "chan"),
            P("chan", None),
            P("chan", None),
            P("chan"),
            P("chan", None),
        ),
        out_specs=(P("seq", "chan"), P("chan", None)),
        check_vma=False,
    )
```

profile of v0, /device:TPU:1, one launch (start us, length us, event | category | flops | bytes accessed | tf_op | source)
XLA Modules:
  0.0 59.7 jit_solution(10305215509680380973)
XLA Ops:
  0.6 0.0 copy-start.1
  0.6 0.8 %copy.8.res_hbm = f32[128,16]{1,0:T(8,128)S(1)} copy(f32[128,16]{0,1:T(8,128)} %param.8) | data formatting | bytes 16384 | tf_op args[2]
  1.5 0.0 copy-start.3
  1.5 0.8 %copy.9.dec_hbm = f32[128,16]{1,0:T(8,128)S(1)} copy(f32[128,16]{0,1:T(8,128)} %param.9) | data formatting | bytes 16384 | tf_op args[3]
  2.3 0.0 copy-done.1
  2.3 0.0 copy-done.3
  2.3 0.0 copy-start
  2.3 1.2 %copy-done = bf16[128,4096]{1,0:T(8,128)(2,1)S(1)} copy-done((bf16[128,4096]{1,0:T(8,128)(2,1)S(1)}, bf16[128,4096]{1,0:T(8,128)(2,1)}, u32[]{:S(2)}) %copy-start) | copy-done | bytes 1048600
  3.5 0.0 copy-start.2
  3.5 0.9 %copy-done.2 = bf16[512,128]{1,0:T(8,128)(2,1)S(1)} copy-done((bf16[512,128]{1,0:T(8,128)(2,1)S(1)}, bf16[512,128]{1,0:T(8,128)(2,1)}, u32[]{:S(2)}) %copy-start.2) | copy-done | bytes 131096
  4.4 53.9 %modal_backward.1 = (bf16[512,128]{1,0:T(8,128)(2,1)S(1)}, f32[128,16]{1,0:T(8,128)S(1)}) custom-call(bf16[512,128]{1,0:T(8,128)(2,1)S(1)} %copy-done.1, bf16[512,128]{1,0:T(8,128)(2,1)S(1)} %copy-done.2, f32[128,16]{1,0:T(8,128)S(1)} %copy.8.res_hbm, f32[128,16]{1,0:T(8,128)S(1)} %copy.9.dec_hbm, f32[1,128]{1,0:T(1,128)S(1)} %bitcast.1, ...), custom_call_target="tpu_custom_call" | custom-call | tf_op jit(solution)/shard_map/modal_backward/pallas_call | solution.py:390
  58.4 0.7 %copy.10 = f32[128,16]{0,1:T(8,128)} copy(f32[128,16]{1,0:T(8,128)S(1)} %get-tuple-element.3) | data formatting | bytes 16384 | tf_op jit(solution)/shard_map/modal_backward/pallas_call | solution.py:390
  59.0 0.7 %copy.12 = bf16[512,128]{1,0:T(8,128)(2,1)} copy(bf16[512,128]{1,0:T(8,128)(2,1)S(1)} %get-tuple-element.6) | data formatting | bytes 262144
Async XLA Ops:
  0.6 1.7 %copy-start.1 = (bf16[512,128]{1,0:T(8,128)(2,1)S(1)}, bf16[512,128]{1,0:T(8,128)(2,1)}, u32[]{:S(2)}) copy-start(bf16[512,128]{1,0:T(8,128)(2,1)} %g_hbm.1) | copy-start | bytes 393220
  1.5 0.8 %copy-start.3 = (f32[128]{0:T(128)S(1)}, f32[128]{0:T(128)}, u32[]{:S(2)}) copy-start(f32[128]{0:T(128)} %param.10) | copy-start | bytes 1540
  2.3 1.2 %copy-start = (bf16[128,4096]{1,0:T(8,128)(2,1)S(1)}, bf16[128,4096]{1,0:T(8,128)(2,1)}, u32[]{:S(2)}) copy-start(bf16[128,4096]{1,0:T(8,128)(2,1)} %w_hbm.1) | copy-start | bytes 3145732
  3.5 0.9 %copy-start.2 = (bf16[512,128]{1,0:T(8,128)(2,1)S(1)}, bf16[512,128]{1,0:T(8,128)(2,1)}, u32[]{:S(2)}) copy-start(bf16[512,128]{1,0:T(8,128)(2,1)} %act_hbm.1) | copy-start | bytes 393220
where the time goes:
time: 59.9 us; the launch traced here: 59.7 us
  Pallas kernels  53.9 us (90%)
  local copies, waits for them, and re-layouts  5.09 us (8%)
  between operations  0.67 us (1%)
    pallas_call x1, Pallas kernels, per_device(): pl.pallas_call(functools.partial(kernel, nseq, nz, 1.0 / math.sqrt(nseq *...  53.9 us
    unnamed x11, local copies, waits for them, and re-layouts  4.42 us

commit v1 on v0

v1 whole, which is shorter than its diff:
```python
import functools
import math

import jax
import jax.numpy as jnp
from jax import lax
from jax.experimental import pallas as pl
from jax.experimental.pallas import tpu as pltpu
from jax.sharding import PartitionSpec as P

MESH = pl.DeviceIdType.MESH
SUB = 8
PIECES = 4


def kernel(
    nseq,
    nz,
    scale_len,
    g_hbm,
    act_hbm,
    res_hbm,
    dec_hbm,
    skip_hbm,
    w_hbm,
    out_ref,
    rg_ref,
    gath,
    w_v,
    g_b,
    act_b,
    res_v,
    dec_v,
    skip_v,
    g_f,
    act_f,
    y_f,
    acc,
    send_acc,
    inbox,
    nat,
    a_bc,
    r_bc,
    z_bc,
    l_bc,
    b_bc,
    c_bc,
    states,
    parts,
    load_sem,
    w_sem,
    w_send,
    w_recv,
    st_send,
    st_recv,
    pt_send,
    pt_recv,
    ring_send,
    ring_recv,
    pr_send,
    pr_recv,
    in_send,
    in_recv,
):
    rows, lanes = g_b.shape
    orders = dec_v.shape[0]
    features = w_hbm.shape[0]
    steps = rows // SUB
    half = nz // 2
    piece = rows // PIECES
    me_s = lax.axis_index("seq")
    me_c = lax.axis_index("chan")
    me_z = me_c // 2
    core = me_c % 2
    partner = me_z * 2 + (1 - core)
    onward = ((me_z + nz + 1 - 2 * core) % nz) * 2 + core
    source = ((me_z + nz - 1 + 2 * core) % nz) * 2 + core

    def chip_at(s, side=core):
        return (me_z + nz + (2 * side - 1) * s) % nz

    def load(src, dst, index):
        return pltpu.make_async_copy(src, dst, load_sem.at[index])

    loads = [
        load(g_hbm, g_b, 0),
        load(dec_hbm, dec_v, 1),
        load(res_hbm, res_v, 2),
        load(skip_hbm, skip_v, 3),
        load(act_hbm, act_b, 4),
    ]
    barrier = pltpu.get_barrier_semaphore()
    for hop in range(1, nseq):
        pl.semaphore_signal(
            barrier, inc=1, device_id=((me_s + hop) % nseq, me_c), device_id_type=MESH
        )
    for other in (partner, source):
        pl.semaphore_signal(barrier, inc=1, device_id=(me_s, other), device_id_type=MESH)
    for copy in loads:
        copy.start()

    def chip_columns(chip):
        return pl.ds(pl.multiple_of(chip * 2 * lanes, 2 * lanes), 2 * lanes)

    def own_weight(s):
        return pltpu.make_async_copy(
            w_hbm.at[:, chip_columns(chip_at(s))], w_v.at[s, pl.ds(0, features), :], w_sem.at[s]
        )

    def partner_weight(s):
        return pltpu.make_async_remote_copy(
            src_ref=w_hbm.at[:, chip_columns(chip_at(s, 1 - core))],
            dst_ref=w_v.at[s, pl.ds(features, features), :],
            send_sem=w_send.at[s],
            recv_sem=w_recv.at[s],
            device_id=(me_s, partner),
            device_id_type=MESH,
        )

    for s in range(half + 1):
        own_weight(s).start()

    loads[1].wait()
    loads[2].wait()
    loads[3].wait()
    decay = dec_v[...]
    strength = res_v[...] * jnp.sqrt(2.0 * decay)
    pole = jnp.exp(-decay)
    for n in range(orders):
        a_bc[n] = jnp.broadcast_to(pole[n : n + 1], (SUB, lanes))
        r_bc[n] = jnp.broadcast_to(strength[n : n + 1], (SUB, lanes))
    acc[...] = jnp.zeros_like(acc)
    send_acc[...] = jnp.zeros_like(send_acc)

    loads[0].wait()
    loads[4].wait()
    g_f[...] = g_b[...].astype(jnp.float32)
    act_f[...] = act_b[...].astype(jnp.float32)

    zero = jnp.zeros((SUB, lanes), jnp.float32)
    skip_row = jnp.broadcast_to(skip_v[...], (SUB, lanes))
    group = orders // 2
    unroll = 2
    for part in range(2):
        chosen = range(part * group, (part + 1) * group)
        poles = [a_bc[n] for n in chosen]
        gains = [r_bc[n] for n in chosen]

        def scan(index, carry, poles=poles, gains=gains, part=part):
            state, total = list(carry[0]), list(carry[1])
            for inner in range(unroll):
                k = index * unroll + inner
                g_row = g_f[pl.ds(steps - 1 - k, SUB, stride=steps), :]
                act_row = act_f[pl.ds(steps - 1 - k, SUB, stride=steps), :]
                where = pl.ds(pl.multiple_of(k * SUB, SUB), SUB)
                y = skip_row * g_row if part == 0 else y_f[where, :]
                terms = []
                for m in range(group):
                    state[m] = g_row + poles[m] * state[m]
                    terms.append(gains[m] * state[m])
                    total[m] = total[m] + act_row * state[m]
                while len(terms) > 1:
                    terms = [terms[i] + terms[i + 1] for i in range(0, len(terms), 2)]
                y_f[where, :] = y + terms[0]
            return tuple(state), tuple(total)

        state, total = lax.fori_loop(
            0, steps // unroll, scan, ((zero,) * group, (zero,) * group)
        )
        for m, n in enumerate(chosen):
            z_bc[n] = state[m]
            l_bc[n] = total[m]

    row = lax.broadcasted_iota(jnp.int32, (SUB, lanes), 0)
    for n in range(orders):
        rate = jnp.broadcast_to(dec_v[n : n + 1, :], (SUB, lanes))
        state = z_bc[n]
        shift = 1
        while shift < SUB:
            moved = jnp.where(row < SUB - shift, pltpu.roll(state, SUB - shift, 0), 0.0)
            state = state + jnp.exp(rate * float(-steps * shift)) * moved
            shift *= 2
        states[me_s, n : n + 1, :] = state[0:1]
        z_bc[n] = jnp.where(row < SUB - 1, pltpu.roll(state, SUB - 1, 0), 0.0)

    pl.semaphore_wait(barrier, nseq - 1 + 2)

    def to_peer(buffer, send, recv, hop):
        peer = (me_s + hop) % nseq
        return pltpu.make_async_remote_copy(
            src_ref=buffer.at[me_s],
            dst_ref=buffer.at[me_s],
            send_sem=send.at[hop],
            recv_sem=recv.at[me_s],
            device_id=(peer, me_c),
            device_id_type=MESH,
        )

    def from_peer(buffer, send, recv, hop):
        peer = (me_s + hop) % nseq
        return pltpu.make_async_remote_copy(
            src_ref=buffer.at[peer],
            dst_ref=buffer.at[peer],
            send_sem=send.at[hop],
            recv_sem=recv.at[peer],
            device_id=(peer, me_c),
            device_id_type=MESH,
        )

    for hop in range(1, nseq):
        to_peer(states, st_send, st_recv, hop).start()
    for s in range(half + 1):
        partner_weight(s).start()

    def weigh(index, carry):
        carry = list(carry)
        for inner in range(unroll):
            j = index * unroll + inner
            act_row = act_f[pl.ds(j, SUB, stride=steps), :]
            for n in range(orders):
                carry[n] = a_bc[n] * (carry[n] + act_row)
        return tuple(carry)

    weights = lax.fori_loop(0, steps // unroll, weigh, (zero,) * orders)
    distance = (SUB - 1 - row).astype(jnp.float32) * float(steps)
    for n in range(orders):
        b_bc[n] = weights[n]
        rate = jnp.broadcast_to(dec_v[n : n + 1, :], (SUB, lanes))
        c_bc[n] = jnp.exp(-rate * distance)
    block_pole = jnp.exp(dec_v[...] * float(-rows))

    for hop in range(1, nseq):
        from_peer(states, st_send, st_recv, hop).wait_recv()
    enter = jnp.zeros((orders, lanes), jnp.float32)
    for later in range(nseq - 1, 0, -1):
        enter = jnp.where(later > me_s, states[later] + block_pole * enter, enter)
    for n in range(orders):
        c_bc[n] = z_bc[n] + c_bc[n] * jnp.broadcast_to(enter[n : n + 1], (SUB, lanes))

    def rows_of(p):
        return pl.ds(pl.multiple_of(p * piece, piece), piece)

    def pass_on(chip, side, s, p):
        view = gath.at[chip * 2 + side, rows_of(p), :]
        return pltpu.make_async_remote_copy(
            src_ref=view,
            dst_ref=view,
            send_sem=ring_send.at[s, side, p],
            recv_sem=ring_recv.at[s, side, p],
            device_id=(me_s, onward),
            device_id_type=MESH,
        )

    def across(side, p):
        view = gath.at[me_z * 2 + side, rows_of(p), :]
        return pltpu.make_async_remote_copy(
            src_ref=view,
            dst_ref=view,
            send_sem=pr_send.at[p],
            recv_sem=pr_recv.at[p],
            device_id=(me_s, partner),
            device_id_type=MESH,
        )

    def hand_over(p):
        return pltpu.make_async_remote_copy(
            src_ref=send_acc.at[rows_of(p), :],
            dst_ref=inbox.at[rows_of(p), :],
            send_sem=in_send.at[p],
            recv_sem=in_recv.at[p],
            device_id=(me_s, partner),
            device_id_type=MESH,
        )

    poles = [a_bc[n] for n in range(orders)]
    entering = tuple(r_bc[n] * c_bc[n] for n in range(orders))

    def finish(p, carry):
        def pair(index, carry):
            ys = []
            for inner in range(2):
                k = p * (piece // SUB) + index * 2 + inner
                carry = [poles[n] * carry[n] for n in range(orders)]
                terms = list(carry)
                while len(terms) > 1:
                    terms = [terms[i] + terms[i + 1] for i in range(0, len(terms), 2)]
                ys.append(y_f[pl.ds(pl.multiple_of(k * SUB, SUB), SUB), :] + terms[0])
            start = pl.multiple_of(p * piece + index * 2 * SUB, 2 * SUB)
            both = jnp.concatenate(ys, axis=0).astype(jnp.bfloat16)
            gath[me_c, pl.ds(start, 2 * SUB), :] = both
            return tuple(carry)

        carry = lax.fori_loop(0, piece // SUB // 2, pair, carry)
        pass_on(me_z, core, 1, p).start()
        across(core, p).start()
        return carry

    lax.fori_loop(0, PIECES, finish, entering)

    for n in range(orders):
        parts[me_s, n : n + 1, :] = jnp.sum(
            l_bc[n] + b_bc[n] * c_bc[n], axis=0, keepdims=True
        )
    for hop in range(1, nseq):
        to_peer(parts, pt_send, pt_recv, hop).start()

    for p in range(PIECES):
        across(1 - core, p).wait_recv()
        pass_on(me_z, 1 - core, 1, p).start()
    for s in range(half + 1):
        own_weight(s).wait()
        partner_weight(s).wait_recv()

    def multiply(s, p):
        chip = chip_at(s)
        where = rows_of(p)
        block = jnp.concatenate([gath[chip * 2, where, :], gath[chip * 2 + 1, where, :]], axis=1)
        both = lax.dot_general(
            block, w_v[s], (((1,), (1,)), ((), ())), preferred_element_type=jnp.float32
        )
        acc[where, :] += both[:, :features]
        send_acc[where, :] += both[:, features:]

    def ring_step(s, _):
        chip = chip_at(s)
        for turn in range(2):
            side = core if turn == 0 else 1 - core
            for p in range(PIECES):
                pass_on(chip, side, s, p).wait_recv()

                @pl.when((s < half - 1) | (p // (PIECES // 2) == core))
                def _(side=side, p=p):
                    pass_on(chip, side, s + 1, p).start()

                index = turn * PIECES + p
                if index % 2 == 1:
                    u = index // 2

                    @pl.when((s >= 2) | (u // (PIECES // 2) == core))
                    def _(u=u):
                        multiply(s - 1, u)

        return 0

    lax.fori_loop(1, half, ring_step, 0)

    ours = [core * (PIECES // 2) + i for i in range(PIECES // 2)]
    theirs = [(1 - core) * (PIECES // 2) + i for i in range(PIECES // 2)]
    for p in theirs:
        multiply(half - 1, p)
    for p in theirs:
        hand_over(p).start()
    for p in ours:
        multiply(half - 1, p)

    for hop in range(1, nseq):
        from_peer(parts, pt_send, pt_recv, hop).wait_recv()
    total = parts[0]
    for other in range(1, nseq):
        total = total + parts[other]
    rg_ref[...] = total * jnp.sqrt(2.0 * dec_v[...]) * scale_len

    far = chip_at(half)
    for p in ours:
        pass_on(far, core, half, p).wait_recv()
    for p in ours:
        pass_on(far, 1 - core, half, p).wait_recv()
        multiply(half, p)
        hand_over(p).start()

    def deliver(p):
        hand_over(p).wait_recv()
        span = piece // SUB
        for i in range(span):
            k = p * span + i
            where = pl.ds(pl.multiple_of(k * SUB, SUB), SUB)
            nat[pl.ds(steps - 1 - k, SUB, stride=steps), :] = acc[where, :] + inbox[where, :]
        for b in range(SUB):
            where = pl.ds(pl.multiple_of(b * steps + steps - (p + 1) * span, span), span)
            out_ref[where, :] = nat[where, :].astype(out_ref.dtype)

    for p in ours + theirs:
        deliver(p)

    for hop in range(1, nseq):
        to_peer(states, st_send, st_recv, hop).wait_send()
        to_peer(parts, pt_send, pt_recv, hop).wait_send()
    for s in range(half + 1):
        partner_weight(s).wait_send()
    for p in range(PIECES):
        across(core, p).wait_send()
        hand_over(p).wait_send()

    def drain(s, _):
        for side in range(2):
            for p in range(PIECES):
                pass_on(me_z, side, s, p).wait_send()
        return 0

    lax.fori_loop(1, half, drain, 0)
    for side in range(2):
        for p in ours:
            pass_on(me_z, side, half, p).wait_send()


def per_device(nseq, nz, grad_out, activation, residues, decay, skip, in_weight):
    rows, lanes = grad_out.shape
    orders = decay.shape[1]
    features, width = in_weight.shape
    f32, bf16 = jnp.float32, jnp.bfloat16
    half = nz // 2
    dma = pltpu.SemaphoreType.DMA
    hbm_spec = pl.BlockSpec(memory_space=pltpu.HBM)
    vmem_spec = pl.BlockSpec(memory_space=pltpu.VMEM)
    spread = pltpu.VMEM((orders, SUB, lanes), f32)
    total = pltpu.VMEM((rows, features), f32)
    arrays = (grad_out, activation, residues.T, decay.T, skip.reshape(1, lanes), in_weight)
    input_grad, residue_grad = pl.pallas_call(
        functools.partial(kernel, nseq, nz, 1.0 / math.sqrt(nseq * rows)),
        out_shape=(
            jax.ShapeDtypeStruct((rows, features), bf16),
            jax.ShapeDtypeStruct((orders, lanes), f32),
        ),
        in_specs=[hbm_spec] * 6,
        out_specs=(vmem_spec, vmem_spec),
        scratch_shapes=[
            pltpu.VMEM((nz * 2, rows, lanes), bf16),
            pltpu.VMEM((half + 1, 2 * features, 2 * lanes), bf16),
            pltpu.VMEM((rows, lanes), bf16),
            pltpu.VMEM((rows, lanes), bf16),
            pltpu.VMEM((orders, lanes), f32),
            pltpu.VMEM((orders, lanes), f32),
            pltpu.VMEM((1, lanes), f32),
            pltpu.VMEM((rows, lanes), f32),
            pltpu.VMEM((rows, lanes), f32),
            pltpu.VMEM((rows, lanes), f32),
            total,
            total,
            total,
            total,
            spread,
            spread,
            spread,
            spread,
            spread,
            spread,
            pltpu.VMEM((nseq, orders, lanes), f32),
            pltpu.VMEM((nseq, orders, lanes), f32),
            dma((5,)),
            dma((half + 1,)),
            dma((half + 1,)),
            dma((half + 1,)),
            dma((nseq,)),
            dma((nseq,)),
            dma((nseq,)),
            dma((nseq,)),
            dma((half + 1, 2, PIECES)),
            dma((half + 1, 2, PIECES)),
            dma((PIECES,)),
            dma((PIECES,)),
            dma((PIECES,)),
            dma((PIECES,)),
        ],
        compiler_params=pltpu.CompilerParams(
            collective_id=0, has_side_effects=True, vmem_limit_bytes=40 * 2**20
        ),
        name="modal_backward",
    )(*(pltpu.with_memory_space_constraint(x, pltpu.HBM) for x in arrays))
    return (input_grad, residue_grad.T)


def solution(mesh):
    nseq = mesh.shape["seq"]
    nz = mesh.shape["chan"] // 2
    return jax.shard_map(
        functools.partial(per_device, nseq, nz),
        mesh=mesh,
        in_specs=(
            P("seq", "chan"),
            P("seq", "chan"),
            P("chan", None),
            P("chan", None),
            P("chan"),
            P("chan", None),
        ),
        out_specs=(P("seq", "chan"), P("chan", None)),
        check_vma=False,
    )
```

time: 59.9 us -> 53.6 us (0.89)
  local copies, waits for them, and re-layouts: 5.09 us -> 1.26 us
  Pallas kernels: 53.9 us -> 51.6 us
    unnamed x11 -> x2, local copies, waits for them, and re-layouts: 4.42 us -> 1.26 us
    pallas_call x1, Pallas kernels: 53.9 us -> 51.6 us  [per_device(): pl.pallas_call(functools.partial(kernel, nseq, nz, 1.0 / math.sqrt(nseq *...]
    pallas_call x1 -> x0, local copies, waits for them, and re-layouts: 0.67 us -> none  [per_device(): pl.pallas_call(functools.partial(kernel, nseq, nz, 1.0 / math.sqrt(nseq *...]
where the time goes in v1:
time: 53.6 us; the launch traced here: 53.5 us
  Pallas kernels  51.6 us (96%)
  local copies, waits for them, and re-layouts  1.26 us (2%)
  between operations  0.64 us (1%)
    pallas_call x1, Pallas kernels, per_device(): pl.pallas_call(functools.partial(kernel, nseq, nz, 1.0 / math.sqrt(nseq *...  51.6 us
    unnamed x2, local copies, waits for them, and re-layouts  1.26 us

profile of v1, /device:TPU:1, one launch (start us, length us, event | category | flops | bytes accessed | tf_op | source)
XLA Modules:
  0.0 53.5 jit_solution(15973231455668838198)
XLA Ops:
  0.6 51.6 %modal_backward.1 = (bf16[512,128]{1,0:T(8,128)(2,1)S(1)}, f32[16,128]{1,0:T(8,128)S(1)}) custom-call(bf16[512,128]{1,0:T(8,128)(2,1)} %g_hbm.1, bf16[512,128]{1,0:T(8,128)(2,1)} %act_hbm.1, f32[16,128]{1,0:T(8,128)} %bitcast.5, f32[16,128]{1,0:T(8,128)} %bitcast.6, f32[1,128]{1,0:T(1,128)} %bitcast.7, bf16[128,4096]{1,0:T(8,128)(2,1)} %w_hbm.1), custom_call_target="tpu_custom_call" | custom-call | tf_op jit(solution)/shard_map/modal_backward/pallas_call | solution.py:418
  52.2 0.7 %copy.10 = bf16[512,128]{1,0:T(8,128)(2,1)} copy(bf16[512,128]{1,0:T(8,128)(2,1)S(1)} %get-tuple-element.8) | data formatting | bytes 262144
  52.9 0.6 %copy.11 = f32[128,16]{0,1:T(8,128)} copy(f32[128,16]{0,1:T(8,128)S(1)} %bitcast.4) | data formatting | bytes 16384

commit v2 on v1

--- a/solution.py
+++ b/solution.py
@@ -11,6 +11,16 @@
 MESH = pl.DeviceIdType.MESH
 SUB = 8
 PIECES = 4
+
+
+def far_first(nseq):
+    edge = max(math.isqrt(nseq), 1)
+
+    def away(hop):
+        across, along = divmod(hop, edge)
+        return min(across, edge - across) + min(along, edge - along)
+
+    return sorted(range(1, nseq), key=lambda hop: -away(hop))
 
 
 def kernel(
@@ -45,6 +55,7 @@
     l_bc,
     b_bc,
     c_bc,
+    e_bc,
     states,
     parts,
     load_sem,
@@ -90,14 +101,23 @@
         load(act_hbm, act_b, 4),
     ]
     barrier = pltpu.get_barrier_semaphore()
-    for hop in range(1, nseq):
-        pl.semaphore_signal(
-            barrier, inc=1, device_id=((me_s + hop) % nseq, me_c), device_id_type=MESH
-        )
-    for other in (partner, source):
+    loads[0].start()
+    loads[1].start()
+    loads[2].start()
+    states[...] = jnp.zeros_like(states)
+    hops = far_first(nseq)
+    for hop in hops:
+
+        @pl.when((me_s + hop) % nseq > me_s)
+        def _(hop=hop):
+            pl.semaphore_signal(
+                barrier, inc=1, device_id=((me_s + hop) % nseq, me_c), device_id_type=MESH
+            )
+
+    for other in (source, partner):
         pl.semaphore_signal(barrier, inc=1, device_id=(me_s, other), device_id_type=MESH)
-    for copy in loads:
-        copy.start()
+    loads[3].start()
+    loads[4].start()
 
     def chip_columns(chip):
         return pl.ds(pl.multiple_of(chip * 2 * lanes, 2 * lanes), 2 * lanes)
@@ -119,28 +139,83 @@
 
     for s in range(half + 1):
         own_weight(s).start()
+    acc[...] = jnp.zeros_like(acc)
+    send_acc[...] = jnp.zeros_like(send_acc)
 
     loads[1].wait()
-    loads[2].wait()
-    loads[3].wait()
     decay = dec_v[...]
-    strength = res_v[...] * jnp.sqrt(2.0 * decay)
     pole = jnp.exp(-decay)
     for n in range(orders):
         a_bc[n] = jnp.broadcast_to(pole[n : n + 1], (SUB, lanes))
+
+    zero = jnp.zeros((SUB, lanes), jnp.float32)
+    loads[0].wait()
+    g_f[...] = g_b[...].astype(jnp.float32)
+    unroll = 2
+
+    def gather_states(index, state):
+        for inner in range(unroll):
+            k = index * unroll + inner
+            g_row = g_f[pl.ds(steps - 1 - k, SUB, stride=steps), :]
+            state = [g_row + a_bc[n] * state[n] for n in range(orders)]
+        return tuple(state)
+
+    ends = lax.fori_loop(0, steps // unroll, gather_states, (zero,) * orders)
+
+    row = lax.broadcasted_iota(jnp.int32, (SUB, lanes), 0)
+    for n in range(orders):
+        rate = jnp.broadcast_to(dec_v[n : n + 1, :], (SUB, lanes))
+        state = ends[n]
+        shift = 1
+        while shift < SUB:
+            moved = jnp.where(row < SUB - shift, pltpu.roll(state, SUB - shift, 0), 0.0)
+            state = state + jnp.exp(rate * float(-steps * shift)) * moved
+            shift *= 2
+        states[me_s, n : n + 1, :] = state[0:1]
+        z_bc[n] = jnp.where(row < SUB - 1, pltpu.roll(state, SUB - 1, 0), 0.0)
+
+    pl.semaphore_wait(barrier, me_s + 2)
+
+    def to_peer(buffer, send, recv, hop):
+        peer = (me_s + hop) % nseq
+        return pltpu.make_async_remote_copy(
+            src_ref=buffer.at[me_s],
+            dst_ref=buffer.at[me_s],
+            send_sem=send.at[hop],
+            recv_sem=recv.at[me_s],
+            device_id=(peer, me_c),
+            device_id_type=MESH,
+        )
+
+    def from_peer(buffer, send, recv, hop):
+        peer = (me_s + hop) % nseq
+        return pltpu.make_async_remote_copy(
+            src_ref=buffer.at[peer],
+            dst_ref=buffer.at[peer],
+            send_sem=send.at[hop],
+            recv_sem=recv.at[peer],
+            device_id=(peer, me_c),
+            device_id_type=MESH,
+        )
+
+    for hop in hops:
+
+        @pl.when((me_s + hop) % nseq < me_s)
+        def _(hop=hop):
+            to_peer(states, st_send, st_recv, hop).start()
+
+    for s in range(half + 1):
+        partner_weight(s).start()
+
+    loads[2].wait()
+    loads[3].wait()
+    loads[4].wait()
+    strength = res_v[...] * jnp.sqrt(2.0 * dec_v[...])
+    for n in range(orders):
         r_bc[n] = jnp.broadcast_to(strength[n : n + 1], (SUB, lanes))
-    acc[...] = jnp.zeros_like(acc)
-    send_acc[...] = jnp.zeros_like(send_acc)
-
-    loads[0].wait()
-    loads[4].wait()
-    g_f[...] = g_b[...].astype(jnp.float32)
     act_f[...] = act_b[...].astype(jnp.float32)
-
-    zero = jnp.zeros((SUB, lanes), jnp.float32)
     skip_row = jnp.broadcast_to(skip_v[...], (SUB, lanes))
     group = orders // 2
-    unroll = 2
     for part in range(2):
         chosen = range(part * group, (part + 1) * group)
         poles = [a_bc[n] for n in chosen]
@@ -164,53 +239,11 @@
                 y_f[where, :] = y + terms[0]
             return tuple(state), tuple(total)
 
-        state, total = lax.fori_loop(
+        _, total = lax.fori_loop(
             0, steps // unroll, scan, ((zero,) * group, (zero,) * group)
         )
         for m, n in enumerate(chosen):
-            z_bc[n] = state[m]
             l_bc[n] = total[m]
-
-    row = lax.broadcasted_iota(jnp.int32, (SUB, lanes), 0)
-    for n in range(orders):
-        rate = jnp.broadcast_to(dec_v[n : n + 1, :], (SUB, lanes))
-        state = z_bc[n]
-        shift = 1
-        while shift < SUB:
-            moved = jnp.where(row < SUB - shift, pltpu.roll(state, SUB - shift, 0), 0.0)
-            state = state + jnp.exp(rate * float(-steps * shift)) * moved
-            shift *= 2
-        states[me_s, n : n + 1, :] = state[0:1]
-        z_bc[n] = jnp.where(row < SUB - 1, pltpu.roll(state, SUB - 1, 0), 0.0)
-
-    pl.semaphore_wait(barrier, nseq - 1 + 2)
-
-    def to_peer(buffer, send, recv, hop):
-        peer = (me_s + hop) % nseq
-        return pltpu.make_async_remote_copy(
-            src_ref=buffer.at[me_s],
-            dst_ref=buffer.at[me_s],
-            send_sem=send.at[hop],
-            recv_sem=recv.at[me_s],
-            device_id=(peer, me_c),
-            device_id_type=MESH,
-        )
-
-    def from_peer(buffer, send, recv, hop):
-        peer = (me_s + hop) % nseq
-        return pltpu.make_async_remote_copy(
-            src_ref=buffer.at[peer],
-            dst_ref=buffer.at[peer],
-            send_sem=send.at[hop],
-            recv_sem=recv.at[peer],
-            device_id=(peer, me_c),
-            device_id_type=MESH,
-        )
-
-    for hop in range(1, nseq):
-        to_peer(states, st_send, st_recv, hop).start()
-    for s in range(half + 1):
-        partner_weight(s).start()
 
     def weigh(index, carry):
         carry = list(carry)
@@ -227,13 +260,20 @@
         b_bc[n] = weights[n]
         rate = jnp.broadcast_to(dec_v[n : n + 1, :], (SUB, lanes))
         c_bc[n] = jnp.exp(-rate * distance)
-    block_pole = jnp.exp(dec_v[...] * float(-rows))
-
-    for hop in range(1, nseq):
-        from_peer(states, st_send, st_recv, hop).wait_recv()
-    enter = jnp.zeros((orders, lanes), jnp.float32)
-    for later in range(nseq - 1, 0, -1):
-        enter = jnp.where(later > me_s, states[later] + block_pole * enter, enter)
+    for later in range(1, nseq):
+        blocks = jnp.maximum(later - me_s - 1, 0).astype(jnp.float32) * float(rows)
+        e_bc[later] = jnp.where(later > me_s, jnp.exp(dec_v[...] * -blocks), 0.0)
+
+    for hop in hops:
+
+        @pl.when((me_s + hop) % nseq > me_s)
+        def _(hop=hop):
+            from_peer(states, st_send, st_recv, hop).wait_recv()
+
+    terms = [e_bc[later] * states[later] for later in range(1, nseq)]
+    while len(terms) > 1:
+        terms = [sum(terms[i : i + 2]) for i in range(0, len(terms), 2)]
+    enter = terms[0]
     for n in range(orders):
         c_bc[n] = z_bc[n] + c_bc[n] * jnp.broadcast_to(enter[n : n + 1], (SUB, lanes))
 
@@ -383,8 +423,12 @@
         deliver(p)
 
     for hop in range(1, nseq):
-        to_peer(states, st_send, st_recv, hop).wait_send()
         to_peer(parts, pt_send, pt_recv, hop).wait_send()
+
+        @pl.when((me_s + hop) % nseq < me_s)
+        def _(hop=hop):
+            to_peer(states, st_send, st_recv, hop).wait_send()
+
     for s in range(half + 1):
         partner_weight(s).wait_send()
     for p in range(PIECES):
@@ -401,6 +445,17 @@
     for side in range(2):
         for p in ours:
             pass_on(me_z, side, half, p).wait_send()
+
+
+def put_out(from_input_grad, from_residue_grad, input_grad, residue_grad, sem):
+    copies = [
+        pltpu.make_async_copy(from_input_grad, input_grad, sem.at[0]),
+        pltpu.make_async_copy(from_residue_grad, residue_grad, sem.at[1]),
+    ]
+    for copy in copies:
+        copy.start()
+    for copy in copies:
+        copy.wait()
 
 
 def per_device(nseq, nz, grad_out, activation, residues, decay, skip, in_weight):
@@ -446,6 +501,7 @@
             spread,
             pltpu.VMEM((nseq, orders, lanes), f32),
             pltpu.VMEM((nseq, orders, lanes), f32),
+            pltpu.VMEM((nseq, orders, lanes), f32),
             dma((5,)),
             dma((half + 1,)),
             dma((half + 1,)),
@@ -466,6 +522,18 @@
         ),
         name="modal_backward",
     )(*(pltpu.with_memory_space_constraint(x, pltpu.HBM) for x in arrays))
+    input_grad, residue_grad = pl.pallas_call(
+        put_out,
+        out_shape=(
+            jax.ShapeDtypeStruct((rows, features), bf16),
+            jax.ShapeDtypeStruct((orders, lanes), f32),
+        ),
+        in_specs=[vmem_spec, vmem_spec],
+        out_specs=(hbm_spec, hbm_spec),
+        scratch_shapes=[dma((2,))],
+        compiler_params=pltpu.CompilerParams(vmem_limit_bytes=2**20),
+        name="put_out",
+    )(input_grad, residue_grad)
     return (input_grad, residue_grad.T)
 
 

time: 53.6 us -> 51.3 us (0.957)
  local copies, waits for them, and re-layouts: 1.26 us -> 0 us
  Pallas kernels: 51.6 us -> 50.5 us
    pallas_call x1, Pallas kernels: 51.6 us -> 49.8 us  [per_device(): pl.pallas_call(functools.partial(kernel, nseq, nz, 1.0 / math.sqrt(nseq *...]
    unnamed x2 -> x0, local copies, waits for them, and re-layouts: 1.26 us -> none
    pallas_call x0 -> x1, Pallas kernels: none -> 0.68 us  [per_device(): pl.pallas_call(put_out, out_shape=(jax.ShapeDtypeStruct((rows, features),...]
where the time goes in v2:
time: 51.3 us; the launch traced here: 51.2 us
  Pallas kernels  50.5 us (98%)
  between operations  0.64 us (1%)
    pallas_call x1, Pallas kernels, per_device(): pl.pallas_call(functools.partial(kernel, nseq, nz, 1.0 / math.sqrt(nseq *...  49.8 us

profile of v2, /device:TPU:1, one launch (start us, length us, event | category | flops | bytes accessed | tf_op | source)
XLA Modules:
  0.0 51.2 jit_solution(16173009831147805765)
XLA Ops:
  0.6 49.8 %modal_backward.1 = (bf16[512,128]{1,0:T(8,128)(2,1)S(1)}, f32[16,128]{1,0:T(8,128)S(1)}) custom-call(bf16[512,128]{1,0:T(8,128)(2,1)} %g_hbm.1, bf16[512,128]{1,0:T(8,128)(2,1)} %act_hbm.1, f32[16,128]{1,0:T(8,128)} %bitcast.4, f32[16,128]{1,0:T(8,128)} %bitcast.5, f32[1,128]{1,0:T(1,128)} %bitcast.6, bf16[128,4096]{1,0:T(8,128)(2,1)} %w_hbm.1), custom_call_target="tpu_custom_call" | custom-call | tf_op jit(solution)/shard_map/modal_backward/pallas_call | solution.py:473
  50.5 0.7 %put_out.1 = (bf16[512,128]{1,0:T(8,128)(2,1)}, f32[16,128]{1,0:T(8,128)}) custom-call(bf16[512,128]{1,0:T(8,128)(2,1)S(1)} %get-tuple-element.6.from_input_grad, f32[16,128]{1,0:T(8,128)S(1)} %get-tuple-element.7.from_residue_grad), custom_call_target="tpu_custom_call" | custom-call | tf_op jit(solution)/shard_map/put_out/pallas_call | solution.py:525

commit v3 on v2

--- a/solution.py
+++ b/solution.py
@@ -10,7 +10,12 @@
 
 MESH = pl.DeviceIdType.MESH
 SUB = 8
+TILT = 0
 PIECES = 4
+
+
+def reach_up(nz):
+    return max((nz - 1) // 2 - TILT, 1)
 
 
 def far_first(nseq):
@@ -77,7 +82,8 @@
     orders = dec_v.shape[0]
     features = w_hbm.shape[0]
     steps = rows // SUB
-    half = nz // 2
+    ups = reach_up(nz)
+    most = max(ups, nz - 1 - ups)
     piece = rows // PIECES
     me_s = lax.axis_index("seq")
     me_c = lax.axis_index("chan")
@@ -86,6 +92,8 @@
     partner = me_z * 2 + (1 - core)
     onward = ((me_z + nz + 1 - 2 * core) % nz) * 2 + core
     source = ((me_z + nz - 1 + 2 * core) % nz) * 2 + core
+
+    last = ups + (nz - 1 - 2 * ups) * core
 
     def chip_at(s, side=core):
         return (me_z + nz + (2 * side - 1) * s) % nz
@@ -137,7 +145,7 @@
             device_id_type=MESH,
         )
 
-    for s in range(half + 1):
+    for s in range(most + 1):
         own_weight(s).start()
     acc[...] = jnp.zeros_like(acc)
     send_acc[...] = jnp.zeros_like(send_acc)
@@ -204,7 +212,7 @@
         def _(hop=hop):
             to_peer(states, st_send, st_recv, hop).start()
 
-    for s in range(half + 1):
+    for s in range(most + 1):
         partner_weight(s).start()
 
     loads[2].wait()
@@ -347,7 +355,7 @@
     for p in range(PIECES):
         across(1 - core, p).wait_recv()
         pass_on(me_z, 1 - core, 1, p).start()
-    for s in range(half + 1):
+    for s in range(most + 1):
         own_weight(s).wait()
         partner_weight(s).wait_recv()
 
@@ -367,10 +375,7 @@
             side = core if turn == 0 else 1 - core
             for p in range(PIECES):
                 pass_on(chip, side, s, p).wait_recv()
-
-                @pl.when((s < half - 1) | (p // (PIECES // 2) == core))
-                def _(side=side, p=p):
-                    pass_on(chip, side, s + 1, p).start()
+                pass_on(chip, side, s + 1, p).start()
 
                 index = turn * PIECES + p
                 if index % 2 == 1:
@@ -382,16 +387,7 @@
 
         return 0
 
-    lax.fori_loop(1, half, ring_step, 0)
-
-    ours = [core * (PIECES // 2) + i for i in range(PIECES // 2)]
-    theirs = [(1 - core) * (PIECES // 2) + i for i in range(PIECES // 2)]
-    for p in theirs:
-        multiply(half - 1, p)
-    for p in theirs:
-        hand_over(p).start()
-    for p in ours:
-        multiply(half - 1, p)
+    lax.fori_loop(1, last, ring_step, 0)
 
     for hop in range(1, nseq):
         from_peer(parts, pt_send, pt_recv, hop).wait_recv()
@@ -400,12 +396,17 @@
         total = total + parts[other]
     rg_ref[...] = total * jnp.sqrt(2.0 * dec_v[...]) * scale_len
 
-    far = chip_at(half)
-    for p in ours:
-        pass_on(far, core, half, p).wait_recv()
-    for p in ours:
-        pass_on(far, 1 - core, half, p).wait_recv()
-        multiply(half, p)
+    far = chip_at(last)
+    for p in range(PIECES):
+        pass_on(far, core, last, p).wait_recv()
+
+        @pl.when((last >= 2) | (p // (PIECES // 2) == core))
+        def _(p=p):
+            multiply(last - 1, p)
+
+    for p in range(PIECES):
+        pass_on(far, 1 - core, last, p).wait_recv()
+        multiply(last, p)
         hand_over(p).start()
 
     def deliver(p):
@@ -419,7 +420,7 @@
             where = pl.ds(pl.multiple_of(b * steps + steps - (p + 1) * span, span), span)
             out_ref[where, :] = nat[where, :].astype(out_ref.dtype)
 
-    for p in ours + theirs:
+    for p in range(PIECES):
         deliver(p)
 
     for hop in range(1, nseq):
@@ -429,7 +430,7 @@
         def _(hop=hop):
             to_peer(states, st_send, st_recv, hop).wait_send()
 
-    for s in range(half + 1):
+    for s in range(most + 1):
         partner_weight(s).wait_send()
     for p in range(PIECES):
         across(core, p).wait_send()
@@ -441,10 +442,7 @@
                 pass_on(me_z, side, s, p).wait_send()
         return 0
 
-    lax.fori_loop(1, half, drain, 0)
-    for side in range(2):
-        for p in ours:
-            pass_on(me_z, side, half, p).wait_send()
+    lax.fori_loop(1, last + 1, drain, 0)
 
 
 def put_out(from_input_grad, from_residue_grad, input_grad, residue_grad, sem):
@@ -463,7 +461,8 @@
     orders = decay.shape[1]
     features, width = in_weight.shape
     f32, bf16 = jnp.float32, jnp.bfloat16
-    half = nz // 2
+    ups = reach_up(nz)
+    most = max(ups, nz - 1 - ups)
     dma = pltpu.SemaphoreType.DMA
     hbm_spec = pl.BlockSpec(memory_space=pltpu.HBM)
     vmem_spec = pl.BlockSpec(memory_space=pltpu.VMEM)
@@ -480,7 +479,7 @@
         out_specs=(vmem_spec, vmem_spec),
         scratch_shapes=[
             pltpu.VMEM((nz * 2, rows, lanes), bf16),
-            pltpu.VMEM((half + 1, 2 * features, 2 * lanes), bf16),
+            pltpu.VMEM((most + 1, 2 * features, 2 * lanes), bf16),
             pltpu.VMEM((rows, lanes), bf16),
             pltpu.VMEM((rows, lanes), bf16),
             pltpu.VMEM((orders, lanes), f32),
@@ -503,15 +502,15 @@
             pltpu.VMEM((nseq, orders, lanes), f32),
             pltpu.VMEM((nseq, orders, lanes), f32),
             dma((5,)),
-            dma((half + 1,)),
-            dma((half + 1,)),
-            dma((half + 1,)),
+            dma((most + 1,)),
+            dma((most + 1,)),
+            dma((most + 1,)),
             dma((nseq,)),
             dma((nseq,)),
             dma((nseq,)),
             dma((nseq,)),
-            dma((half + 1, 2, PIECES)),
-            dma((half + 1, 2, PIECES)),
+            dma((most + 1, 2, PIECES)),
+            dma((most + 1, 2, PIECES)),
             dma((PIECES,)),
             dma((PIECES,)),
             dma((PIECES,)),

time: 51.3 us -> 49.1 us (0.957)
  Pallas kernels: 50.5 us -> 48.3 us
    pallas_call x1, Pallas kernels: 49.8 us -> 47.6 us  [per_device(): pl.pallas_call(functools.partial(kernel, nseq, nz, 1.0 / math.sqrt(nseq *...]
where the time goes in v3:
time: 49.1 us; the launch traced here: 48.9 us
  Pallas kernels  48.3 us (98%)
  between operations  0.64 us (1%)
    pallas_call x1, Pallas kernels, per_device(): pl.pallas_call(functools.partial(kernel, nseq, nz, 1.0 / math.sqrt(nseq *...  47.6 us

profile of v3, /device:TPU:1, one launch (start us, length us, event | category | flops | bytes accessed | tf_op | source)
XLA Modules:
  0.0 48.9 jit_solution(14989925852098122465)
XLA Ops:
  0.6 47.6 %modal_backward.1 = (bf16[512,128]{1,0:T(8,128)(2,1)S(1)}, f32[16,128]{1,0:T(8,128)S(1)}) custom-call(bf16[512,128]{1,0:T(8,128)(2,1)} %g_hbm.1, bf16[512,128]{1,0:T(8,128)(2,1)} %act_hbm.1, f32[16,128]{1,0:T(8,128)} %bitcast.4, f32[16,128]{1,0:T(8,128)} %bitcast.5, f32[1,128]{1,0:T(1,128)} %bitcast.6, bf16[128,4096]{1,0:T(8,128)(2,1)} %w_hbm.1), custom_call_target="tpu_custom_call" | custom-call | tf_op jit(solution)/shard_map/modal_backward/pallas_call | solution.py:472
  48.3 0.7 %put_out.1 = (bf16[512,128]{1,0:T(8,128)(2,1)}, f32[16,128]{1,0:T(8,128)}) custom-call(bf16[512,128]{1,0:T(8,128)(2,1)S(1)} %get-tuple-element.6.from_input_grad, f32[16,128]{1,0:T(8,128)S(1)} %get-tuple-element.7.from_residue_grad), custom_call_target="tpu_custom_call" | custom-call | tf_op jit(solution)/shard_map/put_out/pallas_call | solution.py:524

commit v4 on v3

--- a/solution.py
+++ b/solution.py
@@ -14,7 +14,7 @@
 PIECES = 4
 
 
-def reach_up(nz):
+def reach_down(nz):
     return max((nz - 1) // 2 - TILT, 1)
 
 
@@ -82,21 +82,21 @@
     orders = dec_v.shape[0]
     features = w_hbm.shape[0]
     steps = rows // SUB
-    ups = reach_up(nz)
-    most = max(ups, nz - 1 - ups)
+    downs = reach_down(nz)
+    most = max(downs, nz - 1 - downs)
     piece = rows // PIECES
     me_s = lax.axis_index("seq")
     me_c = lax.axis_index("chan")
     me_z = me_c // 2
     core = me_c % 2
     partner = me_z * 2 + (1 - core)
-    onward = ((me_z + nz + 1 - 2 * core) % nz) * 2 + core
-    source = ((me_z + nz - 1 + 2 * core) % nz) * 2 + core
-
-    last = ups + (nz - 1 - 2 * ups) * core
+    onward = ((me_z + nz - 1 + 2 * core) % nz) * 2 + core
+    source = ((me_z + nz + 1 - 2 * core) % nz) * 2 + core
+
+    last = downs + (nz - 1 - 2 * downs) * core
 
     def chip_at(s, side=core):
-        return (me_z + nz + (2 * side - 1) * s) % nz
+        return (me_z + nz + (1 - 2 * side) * s) % nz
 
     def load(src, dst, index):
         return pltpu.make_async_copy(src, dst, load_sem.at[index])
@@ -461,8 +461,8 @@
     orders = decay.shape[1]
     features, width = in_weight.shape
     f32, bf16 = jnp.float32, jnp.bfloat16
-    ups = reach_up(nz)
-    most = max(ups, nz - 1 - ups)
+    downs = reach_down(nz)
+    most = max(downs, nz - 1 - downs)
     dma = pltpu.SemaphoreType.DMA
     hbm_spec = pl.BlockSpec(memory_space=pltpu.HBM)
     vmem_spec = pl.BlockSpec(memory_space=pltpu.VMEM)

time: 49.1 us -> 48.6 us (0.990)
  Pallas kernels: 48.3 us -> 47.8 us
where the time goes in v4:
time: 48.6 us; the launch traced here: 48.5 us
  Pallas kernels  47.8 us (98%)
  between operations  0.64 us (1%)
    pallas_call x1, Pallas kernels, per_device(): pl.pallas_call(functools.partial(kernel, nseq, nz, 1.0 / math.sqrt(nseq *...  47.2 us

profile of v4, /device:TPU:1, one launch (start us, length us, event | category | flops | bytes accessed | tf_op | source)
XLA Modules:
  0.0 48.5 jit_solution(9407753065143870678)
XLA Ops:
  0.6 47.2 %modal_backward.1 = (bf16[512,128]{1,0:T(8,128)(2,1)S(1)}, f32[16,128]{1,0:T(8,128)S(1)}) custom-call(bf16[512,128]{1,0:T(8,128)(2,1)} %g_hbm.1, bf16[512,128]{1,0:T(8,128)(2,1)} %act_hbm.1, f32[16,128]{1,0:T(8,128)} %bitcast.4, f32[16,128]{1,0:T(8,128)} %bitcast.5, f32[1,128]{1,0:T(1,128)} %bitcast.6, bf16[128,4096]{1,0:T(8,128)(2,1)} %w_hbm.1), custom_call_target="tpu_custom_call" | custom-call | tf_op jit(solution)/shard_map/modal_backward/pallas_call | solution.py:472
  47.8 0.7 %put_out.1 = (bf16[512,128]{1,0:T(8,128)(2,1)}, f32[16,128]{1,0:T(8,128)}) custom-call(bf16[512,128]{1,0:T(8,128)(2,1)S(1)} %get-tuple-element.6.from_input_grad, f32[16,128]{1,0:T(8,128)S(1)} %get-tuple-element.7.from_residue_grad), custom_call_target="tpu_custom_call" | custom-call | tf_op jit(solution)/shard_map/put_out/pallas_call | solution.py:524
